TPU v7x, 256 devices: a whole 4x4x8 slice. The times are simulated.
256 devices in a mesh: rows: 64 (over x, z, core), cols: 4 (over y).
Axes of the slice: x: 4, y: 4, z: 8, core: 2. Of those that a mesh axis runs over, the one named last changes fastest.
Arguments:
- block_list: int32 [512, 24], P('rows', 'cols'), may hold values from -1 to 511, as said below
- points: bfloat16 [16, 131072], P(None, 'rows'), may hold values from -4 to 4
- targets: float32 [32, 131072], P(None, 'rows'), may hold values from -6 to 6
Outputs:
- solution: float32 [32, 131072], P(None, 'rows')
- residual: float32 [32, 131072], P(None, 'rows')
Inputs may be any that keep to these rules, and one draw needn't show every extreme that they name: `block_list`: A non-empty entry j of block row i satisfies j <= i. Within the 6 slots of a block row held by one index of cols, the entries lie in different groups of 8 consecutive blocks. Of all slots held by one device (8 block rows of 6 slots), at most 1 name blocks of any one group of 8 consecutive blocks, and in every draw some device reaches 1.
All inputs are finite; a program needn't handle non-finite values.
Results may differ from a plain program's by a relative error of at most 0.0057.
Values may be sent and summed in bfloat16 or wider, within the bound.
A program may use at most 64 MiB of HBM per device.

v0:
```python
import jax
import jax.numpy as jnp
from jax import lax
from jax.sharding import PartitionSpec as P

ITERS = 2
REG = 1.5
RADIUS = 0.25


def wendland(left_x, right_x):
    left_f = left_x.astype(jnp.float32)
    right_f = right_x.astype(jnp.float32)
    left_sq = jnp.sum(left_f * left_f, axis=1)
    right_sq = jnp.sum(right_f * right_f, axis=1)
    inner_prod = jnp.einsum("nda,ndb->nab", left_f, right_f, precision=lax.Precision.HIGHEST)
    dist_sq = left_sq[:, :, None] + right_sq[:, None, :] - 2.0 * inner_prod
    scaled = jnp.sqrt(jnp.maximum(dist_sq, 0.0)) / RADIUS
    remain = jnp.maximum(1.0 - scaled, 0.0)
    square = remain * remain
    return square * square * (4.0 * scaled + 1.0)


def local(block_list, points, targets):
    row_count = lax.axis_size("rows")
    row_index = lax.axis_index("rows")
    block_rows, slot_width = block_list.shape
    coord_dim, npoints = points.shape
    outputs = targets.shape[0]
    block_len = npoints // block_rows
    slot_count = block_rows * slot_width
    capacity = (slot_count + row_count - 1) // row_count
    buffer_len = row_count * capacity
    turn_rows = 4
    turn_count = block_rows // turn_rows
    entries = block_list.reshape(slot_count)
    is_live = entries >= 0
    owners = jnp.where(is_live, entries // block_rows, 0)
    local_idx = jnp.where(is_live, entries - owners * block_rows, 0)
    first_row = row_index * block_rows
    row_global = first_row + jnp.arange(slot_count, dtype=jnp.int32) // slot_width
    off_diag = is_live & (entries != row_global)
    owner_hits = (
        (owners[:, None] == jnp.arange(row_count, dtype=jnp.int32)[None, :]) & is_live[:, None]
    ).astype(jnp.int32)
    slot_rank = jnp.sum((jnp.cumsum(owner_hits, axis=0) - owner_hits) * owner_hits, axis=1)
    place_at = jnp.where(is_live, owners * capacity + slot_rank, buffer_len)
    pick_at = jnp.minimum(place_at, buffer_len - 1)
    wanted = jnp.full((buffer_len,), -1, jnp.int32).at[place_at].set(local_idx, mode="drop")
    askers = jnp.full((buffer_len,), -1, jnp.int32).at[place_at].set(row_global, mode="drop")
    request = jnp.stack([wanted, askers], axis=1).reshape(row_count, capacity, 2)
    incoming = lax.all_to_all(request, "rows", split_axis=0, concat_axis=0, tiled=True).reshape(
        buffer_len, 2
    )
    in_live = incoming[:, 0] >= 0
    in_idx = jnp.maximum(incoming[:, 0], 0)
    collect_map = (
        (in_idx[None, :] == jnp.arange(block_rows, dtype=jnp.int32)[:, None]) & in_live[None, :]
    ).astype(jnp.float32)

    def serve(blocks):
        chosen = jnp.where(in_live[:, None, None], blocks[in_idx], jnp.zeros((), blocks.dtype))
        arrived = lax.all_to_all(
            chosen.reshape(row_count, capacity, blocks.shape[1], block_len),
            "rows",
            split_axis=0,
            concat_axis=0,
            tiled=True,
        )
        gotten = arrived.reshape(buffer_len, blocks.shape[1], block_len)[pick_at]
        return jnp.where(is_live[:, None, None], gotten, jnp.zeros((), gotten.dtype))

    def collect(terms):
        flat = terms.reshape(buffer_len, -1)
        summed = jnp.dot(
            collect_map, flat, precision=lax.Precision.HIGHEST, preferred_element_type=jnp.float32
        )
        return summed.reshape(block_rows, terms.shape[1], block_len)

    def give_back(mirror):
        placed = (
            jnp.zeros((buffer_len,) + mirror.shape[1:], jnp.float32)
            .at[place_at]
            .set(mirror, mode="drop")
        )
        arrived = lax.all_to_all(
            placed.reshape(row_count, capacity, mirror.shape[1], block_len),
            "rows",
            split_axis=0,
            concat_axis=0,
            tiled=True,
        )
        return collect(arrived.reshape(buffer_len, mirror.shape[1], block_len))

    def column_total(partial_value):
        return lax.psum(partial_value, "cols")

    def global_sum(values):
        return lax.psum(values, "rows")

    own_x = points.reshape(coord_dim, block_rows, block_len).transpose(1, 0, 2)
    far_x = serve(own_x)
    grouped_x = own_x.reshape(turn_count, turn_rows, coord_dim, block_len)
    grouped_far = far_x.reshape(turn_count, turn_rows * slot_width, coord_dim, block_len)
    grouped_live = is_live.reshape(turn_count, turn_rows * slot_width)
    grouped_off = off_diag.reshape(turn_count, turn_rows * slot_width)

    def row_pass(own_w, far_w):

        def row_step(pieces):
            near_x, remote_x, live_now, off_now = (pieces[0], pieces[1], pieces[2], pieces[3])
            values = jnp.where(
                live_now[:, None, None],
                wendland(jnp.repeat(near_x, slot_width, axis=0), remote_x),
                0.0,
            )
            if own_w is None:
                direct = jnp.sum(
                    jnp.sum(values, axis=2).reshape(turn_rows, slot_width, block_len), axis=1
                )[:, None, :]
                mirror = jnp.where(off_now[:, None], jnp.sum(values, axis=1), 0.0)[:, None, :]
                return (direct, mirror)
            kernel_bf = values.astype(jnp.bfloat16)
            direct = jnp.einsum(
                "nab,nob->noa", kernel_bf, pieces[5], preferred_element_type=jnp.float32
            )
            direct = jnp.sum(direct.reshape(turn_rows, slot_width, outputs, block_len), axis=1)
            mirror = jnp.einsum(
                "nab,noa->nob",
                kernel_bf,
                jnp.repeat(pieces[4], slot_width, axis=0),
                preferred_element_type=jnp.float32,
            )
            return (direct, jnp.where(off_now[:, None, None], mirror, 0.0))

        pieces = (grouped_x, grouped_far, grouped_live, grouped_off)
        if own_w is not None:
            pieces = pieces + (
                own_w.reshape(turn_count, turn_rows, outputs, block_len),
                far_w.reshape(turn_count, turn_rows * slot_width, outputs, block_len),
            )
        results = lax.map(row_step, pieces)
        channels = results[0].shape[2]
        direct = results[0].reshape(block_rows, channels, block_len)
        return (direct, results[1].reshape(slot_count, channels, block_len))

    direct, mirror = row_pass(None, None)
    degree_part = direct + give_back(mirror)
    inv_root = 1.0 / jnp.sqrt(1.0 + column_total(degree_part))
    resid = targets.reshape(outputs, block_rows, block_len).transpose(1, 0, 2)
    direction = resid
    solution = jnp.zeros_like(resid)
    norm_now = global_sum(jnp.sum(resid * resid, axis=(0, 2)))
    for iteration in range(ITERS):
        weights = (direction * inv_root).astype(jnp.bfloat16)
        apply_far_w = serve(weights)
        apply_direct, apply_mirror = row_pass(weights, apply_far_w)
        apply_partial_value = apply_direct + give_back(apply_mirror)
        applied = REG * direction + inv_root * column_total(apply_partial_value)
        step_size = norm_now / global_sum(jnp.sum(direction * applied, axis=(0, 2)))
        solution = solution + step_size[None, :, None] * direction
        resid = resid - step_size[None, :, None] * applied
        if iteration + 1 < ITERS:
            norm_next = global_sum(jnp.sum(resid * resid, axis=(0, 2)))
            direction = resid + (norm_next / norm_now)[None, :, None] * direction
            norm_now = norm_next
    return (
        solution.transpose(1, 0, 2).reshape(outputs, npoints),
        resid.transpose(1, 0, 2).reshape(outputs, npoints),
    )


def solution(mesh):
    placed = (P("rows", "cols"), P(None, "rows"), P(None, "rows"))
    return jax.shard_map(
        local,
        mesh=mesh,
        in_specs=placed,
        out_specs=(P(None, "rows"), P(None, "rows")),
        check_vma=False,
    )
```

profile of v0, /device:TPU:16, one launch (start us, length us, event | category | flops | bytes accessed | tf_op | source)
XLA Modules:
  0.0 810.2 jit_solution(6442422851500337374)
XLA Ops:
  11.4 11.9 %all-to-all-start = ((s32[64,1,2]{2,1,0:T(1,128)}), s32[64,1,2]{2,1,0:T(1,128)S(1)}, u32[]{:S(2)}, u32[]{:S(2)}) async-start(s32[64,1,2]{2,1,0:T(1,128)} %copy.22), calls=%async_computation | async-start | bytes 65536 | tf_op jit(solution)/shard_map/all_to_all | solution.py:52
  24.2 8.6 %all-to-all-done = s32[64,1,2]{2,1,0:T(1,128)S(1)} async-done(((s32[64,1,2]{2,1,0:T(1,128)}), s32[64,1,2]{2,1,0:T(1,128)S(1)}, u32[]{:S(2)}, u32[]{:S(2)}) %all-to-all-start) | async-done | bytes 544 | tf_op jit(solution)/shard_map/all_to_all | solution.py:52
  34.4 4.6 all-to-all-start.1
  39.1 17.1 %all-to-all-done.1 = bf16[64,1,16,256]{3,2,1,0:T(8,128)(2,1)S(1)} async-done(((bf16[64,1,16,256]{3,2,1,0:T(8,128)(2,1)}), bf16[64,1,16,256]{3,2,1,0:T(8,128)(2,1)S(1)}, u32[]{:S(2)}, u32[]{:S(2)}) %all-to-all-start.1) | async-done | bytes 524320 | tf_op jit(solution)/shard_map/all_to_all | solution.py:63
  56.9 12.5 %while.42 = (s32[]{:T(128)}, f32[2,4,1,256]{3,2,1,0:T(1,128)S(1)}, f32[2,24,1,256]{3,1,2,0:T(8,128)S(1)}, pred[2,24]{1,0:T(4,128)(4,1)S(1)}, bf16[2,4,16,256]{3,...) while((s32[]{:T(128)}, f32[2,4,1,256]{3,2,1,0:T(1,128)S(1)}, ...), condition=%wide.region_12.13_spmd, body=%wide.region_6.12_spmd.sunk | while | flops 74260480 | bytes 1274609 | solution.py:142
  57.2 5.8 fusion.105
  63.4 5.9 fusion.105
  70.9 6.4 all-to-all-start.2
  77.5 9.6 %all-to-all-done.2 = f32[64,1,1,256]{3,2,1,0:T(1,128)S(1)} async-done(((f32[64,1,1,256]{3,2,1,0:T(1,128)}), f32[64,1,1,256]{3,2,1,0:T(1,128)S(1)}, u32[]{:S(2)}, u32[]{:S(2)}) %all-to-all-start.2) | async-done | bytes 65568 | tf_op jit(solution)/shard_map/all_to_all | solution.py:86
  87.2 8.5 %psum.50 = f32[8,1,256]{2,0,1:T(8,128)S(1)} all-reduce(f32[8,1,256]{2,0,1:T(8,128)S(1)} %fusion.37), channel_id=1, replica_groups=mesh['rows'=64,'cols'=4] {'cols'}, use_global_device_ids=true, to_apply=%region_14.15 | all-reduce | flops 2048 | bytes 16384 | tf_op jit(solution)/shard_map/psum | solution.py:96
  97.5 4.7 all-to-all-start.3
  102.3 28.1 %all-to-all-done.3 = bf16[64,1,32,256]{3,2,1,0:T(8,128)(2,1)S(1)} async-done(((bf16[64,1,32,256]{3,2,1,0:T(8,128)(2,1)}), bf16[64,1,32,256]{3,2,1,0:T(8,128)(2,1)S(1)}, u32[]{:S(2)}, u32[]{:S(2)}) %all-to-all-start.3) | async-done | bytes 1048608 | tf_op jit(solution)/shard_map/all_to_all | solution.py:63
  132.5 16.1 %while.43 = (s32[]{:T(128)}, f32[2,4,32,256]{3,2,1,0:T(8,128)S(1)}, f32[2,24,32,256]{3,2,1,0:T(8,128)}, bf16[2,24,32,256]{3,2,1,0:T(8,128)(2,1)S(1)}, pred[2,24]...) while((s32[]{:T(128)}, f32[2,4,32,256]{3,2,1,0:T(8,128)S(1)}, ...), condition=%wide.region_19.20_spmd, body=%wide.region_15.19_spmd.sunk | while | flops 274375680 | bytes 14607621 | solution.py:142
  132.7 5.1 select_convert_fusion.4
  140.8 5.1 select_convert_fusion.4
  146.0 1.5 fusion.114
  148.9 5.1 scatter_fusion
  154.1 57.7 %all_to_all.35 = f32[64,1,32,256]{3,2,1,0:T(8,128)S(1)} all-to-all(f32[64,1,32,256]{3,2,1,0:T(8,128)S(1)} %bitcast.324), channel_id=1, replica_groups=mesh['rows'=64,'cols'=4] {'rows'}, dimensions={0} | all-to-all | bytes 4194304 | tf_op jit(solution)/shard_map/all_to_all | solution.py:86
  211.7 2.7 fusion.31
  214.5 42.9 %all-reduce.4.cloned.1.call-done = f32[8,32,256]{2,0,1:T(8,128)} async-done(((f32[8,32,256]{2,0,1:T(8,128)}), f32[8,32,256]{2,0,1:T(8,128)}) %all-reduce.4.cloned.1.call-update) | async-done | bytes 262160 | tf_op jit(solution)/shard_map/psum | solution.py:96
  258.6 127.0 %all-reduce = (f32[32]{0:T(128)S(1)}, f32[32]{0:T(128)S(1)}) all-reduce(f32[32]{0:T(128)S(1)} %get-tuple-element.383, f32[32]{0:T(128)S(1)} %get-tuple-element.382), channel_id=1, replica_groups=mesh['rows'=64,'cols'=4] {'rows'}, use_global_device_ids=true, to_apply=%region_1.2 | all-reduce | flops 64 | bytes 512 | tf_op jit(solution)/shard_map/psum | solution.py:99
  387.1 124.0 %psum.53 = f32[32]{0:T(128)S(1)} all-reduce(f32[32]{0:T(128)S(1)} %multiply_reduce_fusion.7), channel_id=1, replica_groups=mesh['rows'=64,'cols'=4] {'rows'}, use_global_device_ids=true, to_apply=%region_25.26 | all-reduce | flops 32 | bytes 256 | tf_op jit(solution)/shard_map/psum | solution.py:99
  513.1 32.0 %all_to_all.37 = bf16[64,1,32,256]{3,2,1,0:T(8,128)(2,1)S(1)} all-to-all(bf16[64,1,32,256]{3,2,1,0:T(8,128)(2,1)S(1)} %fusion.38), channel_id=1, replica_groups=mesh['rows'=64,'cols'=4] {'rows'}, dimensions={0} | all-to-all | bytes 2097152 | tf_op jit(solution)/shard_map/all_to_all | solution.py:63
  547.2 16.1 %while.44 = (s32[]{:T(128)}, f32[2,4,32,256]{3,2,1,0:T(8,128)S(1)}, f32[2,24,32,256]{3,2,1,0:T(8,128)}, bf16[2,24,32,256]{3,2,1,0:T(8,128)(2,1)S(1)}, pred[2,24]...) while((s32[]{:T(128)}, f32[2,4,32,256]{3,2,1,0:T(8,128)S(1)}, ...), condition=%wide.region_30.31_spmd, body=%wide.region_26.30_spmd.sunk | while | flops 274375680 | bytes 14607621 | solution.py:142
  547.4 5.1 select_convert_fusion.5
  555.5 5.1 select_convert_fusion.5
  560.7 1.5 fusion.123
  563.6 5.1 scatter_fusion.1
  568.8 57.7 %all_to_all.36 = f32[64,1,32,256]{3,2,1,0:T(8,128)S(1)} all-to-all(f32[64,1,32,256]{3,2,1,0:T(8,128)S(1)} %bitcast.323), channel_id=1, replica_groups=mesh['rows'=64,'cols'=4] {'rows'}, dimensions={0} | all-to-all | bytes 4194304 | tf_op jit(solution)/shard_map/all_to_all | solution.py:86
  626.4 2.7 fusion.34
  629.2 42.9 %all-reduce.6.cloned.1.call-done = f32[8,32,256]{2,0,1:T(8,128)} async-done(((f32[8,32,256]{2,0,1:T(8,128)}), f32[8,32,256]{2,0,1:T(8,128)}) %all-reduce.6.cloned.1.call-update) | async-done | bytes 262160 | tf_op jit(solution)/shard_map/psum | solution.py:96
  673.6 127.0 %psum.55 = f32[32]{0:T(128)S(1)} all-reduce(f32[32]{0:T(128)S(1)} %multiply_reduce_fusion.6), channel_id=1, replica_groups=mesh['rows'=64,'cols'=4] {'rows'}, use_global_device_ids=true, to_apply=%region_34.35 | all-reduce | flops 32 | bytes 256 | tf_op jit(solution)/shard_map/psum | solution.py:99
  (146 shorter events, 33.5 us)
Async XLA Ops:
  7.2 31.9 %copy-start.5 = (s32[8,6]{1,0:T(8,128)S(1)}, s32[8,6]{1,0:T(8,128)}, u32[]{:S(2)}) copy-start(s32[8,6]{1,0:T(8,128)} %param.9) | copy-start | bytes 580
  11.4 21.4 %all-to-all-start = ((s32[64,1,2]{2,1,0:T(1,128)}), s32[64,1,2]{2,1,0:T(1,128)S(1)}, u32[]{:S(2)}, u32[]{:S(2)}) async-start(s32[64,1,2]{2,1,0:T(1,128)} %copy.22), calls=%async_computation | async-start | bytes 65536 | tf_op jit(solution)/shard_map/all_to_all | solution.py:52
  34.4 21.8 %all-to-all-start.1 = ((bf16[64,1,16,256]{3,2,1,0:T(8,128)(2,1)}), bf16[64,1,16,256]{3,2,1,0:T(8,128)(2,1)S(1)}, u32[]{:S(2)}, u32[]{:S(2)}) async-start(bf16[64,1,16,256]{3,2,1,0:T(8,128)(2,1)} %bitcast_select_fusion.2), calls=%async_computation.1 | async-start | bytes 1048576 | tf_op jit(solution)/shard_map/all_to_all | solution.py:63
  56.9 20.4 %copy-start.4 = (f32[32,2048]{1,0:T(8,128)S(1)}, f32[32,2048]{1,0:T(8,128)}, u32[]{:S(2)}) copy-start(f32[32,2048]{1,0:T(8,128)} %param.11) | copy-start | bytes 786436
  70.9 16.2 %all-to-all-start.2 = ((f32[64,1,1,256]{3,2,1,0:T(1,128)}), f32[64,1,1,256]{3,2,1,0:T(1,128)S(1)}, u32[]{:S(2)}, u32[]{:S(2)}) async-start(f32[64,1,1,256]{3,2,1,0:T(1,128)} %reshape.420), calls=%async_computation.2 | async-start | bytes 131072 | tf_op jit(solution)/shard_map/all_to_all | solution.py:86
  77.4 20.1 %copy-start = (f32[4,8,8,256]{3,2,1,0:T(8,128)}, f32[4,8,8,256]{3,2,1,0:T(8,128)S(1)}, u32[]{:S(2)}) copy-start(f32[4,8,8,256]{3,2,1,0:T(8,128)S(1)} %copy.51) | copy-start | bytes 786436
  97.5 32.8 %all-to-all-start.3 = ((bf16[64,1,32,256]{3,2,1,0:T(8,128)(2,1)}), bf16[64,1,32,256]{3,2,1,0:T(8,128)(2,1)S(1)}, u32[]{:S(2)}, u32[]{:S(2)}) async-start(bf16[64,1,32,256]{3,2,1,0:T(8,128)(2,1)} %fusion.39), calls=%async_computation.3 | async-start | bytes 2097152 | tf_op jit(solution)/shard_map/all_to_all | solution.py:63
  102.2 155.1 %all-reduce.4.cloned.1.call-start = ((), (), s32[]{:S(2)}) async-start(), calls=%async_computation.7 | async-start | bytes 524288 | tf_op jit(solution)/shard_map/psum | solution.py:96
  154.1 103.3 %copy-start.1 = (f32[4,8,8,256]{3,2,1,0:T(8,128)S(1)}, f32[4,8,8,256]{3,2,1,0:T(8,128)}, u32[]{:S(2)}) copy-start(f32[4,8,8,256]{3,2,1,0:T(8,128)} %copy-done) | copy-start | bytes 786436
  214.4 457.6 %all-reduce.6.cloned.1.call-start = ((), (), s32[]{:S(2)}) async-start(), calls=%async_computation.8 | async-start | bytes 524288 | tf_op jit(solution)/shard_map/psum | solution.py:96
  568.8 103.3 %copy-start.2 = (f32[4,8,8,256]{3,2,1,0:T(8,128)S(1)}, f32[4,8,8,256]{3,2,1,0:T(8,128)}, u32[]{:S(2)}) copy-start(f32[4,8,8,256]{3,2,1,0:T(8,128)} %copy-done) | copy-start | bytes 786436
  568.8 103.3 %copy-start.3 = (f32[8,32,256]{2,0,1:T(8,128)S(1)}, f32[8,32,256]{2,0,1:T(8,128)}, u32[]{:S(2)}) copy-start(f32[8,32,256]{2,0,1:T(8,128)} %all-reduce.4.cloned.1.call-done) | copy-start | bytes 786436
Sparse Core Ops, SparseCore 0:
  214.5 42.7 all-reduce.3
  629.3 42.7 all-reduce.5
where the time goes:
time: 811 us; the launch traced here: 810 us
  blocking collectives  534 us (66%)
  waiting for transfers between devices  149 us (18%)
  matrix products  47.9 us (6%)
  starting transfers between devices  27.7 us (3%)
  local copies, waits for them, and re-layouts  25.6 us (3%)
  between operations  14.4 us (2%)
  other arithmetic  10.8 us (1%)
    psum x3, blocking collectives, global_sum(): return lax.psum(values, 'rows')  378 us
    all_to_all x2, blocking collectives, give_back(): lax.all_to_all(placed.reshape(row_count, capacity, mirror.shape[1], block...  115 us
    psum x2, waiting for transfers between devices, column_total(): return lax.psum(partial_value, 'cols')  85.8 us
    all_to_all x2, waiting for transfers between devices, serve(): lax.all_to_all(chosen.reshape(row_count, capacity, blocks.shape[1], block...  45.2 us
    dot_general x6, matrix products, wendland(): jnp.einsum('nda,ndb->nab', left_f, right_f, precision=lax.Precision.HIGHEST)  32.3 us
    all_to_all x1, blocking collectives, serve(): lax.all_to_all(chosen.reshape(row_count, capacity, blocks.shape[1], block...  32 us
  transfers between devices with their start and end apart: 6, of which 6 were waited for; matrix products, arithmetic and copies ran while one was open for 0% of the time, Pallas kernels for 0%

commit v1 on v0

--- a/solution.py
+++ b/solution.py
@@ -96,7 +96,7 @@
         return lax.psum(partial_value, "cols")
 
     def global_sum(values):
-        return lax.psum(values, "rows")
+        return jnp.sum(lax.all_gather(values, "rows"), axis=0)
 
     own_x = points.reshape(coord_dim, block_rows, block_len).transpose(1, 0, 2)
     far_x = serve(own_x)

time: 811 us -> 939 us (1.16)
  blocking collectives: 534 us -> 660 us
    unnamed x0 -> x3, blocking collectives: none -> 504 us
    psum x3 -> x0, blocking collectives: 378 us -> none  [global_sum(): return lax.psum(values, 'rows')]
where the time goes in v1:
time: 939 us; the launch traced here: 938 us
  blocking collectives  660 us (70%)
  waiting for transfers between devices  148 us (16%)
  matrix products  48 us (5%)
  local copies, waits for them, and re-layouts  27.7 us (3%)
  starting transfers between devices  27.7 us (3%)
  between operations  15.2 us (2%)
  other arithmetic  10.9 us (1%)
    unnamed x3, blocking collectives  504 us
    all_to_all x2, blocking collectives, give_back(): lax.all_to_all(placed.reshape(row_count, capacity, mirror.shape[1], block...  115 us
    psum x2, waiting for transfers between devices, column_total(): return lax.psum(partial_value, 'cols')  84.4 us
    all_to_all x2, waiting for transfers between devices, serve(): lax.all_to_all(chosen.reshape(row_count, capacity, blocks.shape[1], block...  45.2 us
    dot_general x6, matrix products, wendland(): jnp.einsum('nda,ndb->nab', left_f, right_f, precision=lax.Precision.HIGHEST)  32.3 us
    all_to_all x1, blocking collectives, serve(): lax.all_to_all(chosen.reshape(row_count, capacity, blocks.shape[1], block...  32 us
  transfers between devices with their start and end apart: 6, of which 6 were waited for; matrix products, arithmetic and copies ran while one was open for 0% of the time, Pallas kernels for 0%

profile of v1, /device:TPU:16, one launch (start us, length us, event | category | flops | bytes accessed | tf_op | source)
XLA Modules:
  0.0 937.7 jit_solution(7840834377341587639)
XLA Ops:
  11.4 11.9 %all-to-all-start = ((s32[64,1,2]{2,1,0:T(1,128)}), s32[64,1,2]{2,1,0:T(1,128)S(1)}, u32[]{:S(2)}, u32[]{:S(2)}) async-start(s32[64,1,2]{2,1,0:T(1,128)} %copy.22), calls=%async_computation | async-start | bytes 65536 | tf_op jit(solution)/shard_map/all_to_all | solution.py:52
  24.2 8.6 all-to-all-done
  34.4 4.6 all-to-all-start.1
  39.1 17.1 %all-to-all-done.1 = bf16[64,1,16,256]{3,2,1,0:T(8,128)(2,1)S(1)} async-done(((bf16[64,1,16,256]{3,2,1,0:T(8,128)(2,1)}), bf16[64,1,16,256]{3,2,1,0:T(8,128)(2,1)S(1)}, u32[]{:S(2)}, u32[]{:S(2)}) %all-to-all-start.1) | async-done | bytes 524320 | tf_op jit(solution)/shard_map/all_to_all | solution.py:63
  56.9 12.5 %while.42 = (s32[]{:T(128)}, f32[2,4,1,256]{3,2,1,0:T(1,128)S(1)}, f32[2,24,1,256]{3,1,2,0:T(8,128)S(1)}, pred[2,24]{1,0:T(4,128)(4,1)S(1)}, bf16[2,4,16,256]{3,...) while((s32[]{:T(128)}, f32[2,4,1,256]{3,2,1,0:T(1,128)S(1)}, ...), condition=%wide.region_12.13_spmd, body=%wide.region_6.12_spmd.sunk | while | flops 74260480 | bytes 1274609 | solution.py:142
  57.2 5.9 fusion.105
  63.4 5.9 fusion.105
  70.9 6.4 all-to-all-start.2
  77.5 9.6 %all-to-all-done.2 = f32[64,1,1,256]{3,2,1,0:T(1,128)S(1)} async-done(((f32[64,1,1,256]{3,2,1,0:T(1,128)}), f32[64,1,1,256]{3,2,1,0:T(1,128)S(1)}, u32[]{:S(2)}, u32[]{:S(2)}) %all-to-all-start.2) | async-done | bytes 65568 | tf_op jit(solution)/shard_map/all_to_all | solution.py:86
  87.2 8.5 psum.21
  97.5 4.7 all-to-all-start.3
  102.2 28.1 %all-to-all-done.3 = bf16[64,1,32,256]{3,2,1,0:T(8,128)(2,1)S(1)} async-done(((bf16[64,1,32,256]{3,2,1,0:T(8,128)(2,1)}), bf16[64,1,32,256]{3,2,1,0:T(8,128)(2,1)S(1)}, u32[]{:S(2)}, u32[]{:S(2)}) %all-to-all-start.3) | async-done | bytes 1048608 | tf_op jit(solution)/shard_map/all_to_all | solution.py:63
  132.5 16.1 %while.43 = (s32[]{:T(128)}, f32[2,4,32,256]{3,2,1,0:T(8,128)S(1)}, f32[2,24,32,256]{3,2,1,0:T(8,128)}, bf16[2,24,32,256]{3,2,1,0:T(8,128)(2,1)S(1)}, pred[2,24]...) while((s32[]{:T(128)}, f32[2,4,32,256]{3,2,1,0:T(8,128)S(1)}, ...), condition=%wide.region_19.20_spmd, body=%wide.region_15.19_spmd.sunk | while | flops 274375680 | bytes 14607621 | solution.py:142
  132.7 5.1 select_convert_fusion.4
  140.8 5.1 select_convert_fusion.4
  146.0 1.5 fusion.114
  148.9 5.1 scatter_fusion
  154.1 57.7 %all_to_all.35 = f32[64,1,32,256]{3,2,1,0:T(8,128)S(1)} all-to-all(f32[64,1,32,256]{3,2,1,0:T(8,128)S(1)} %bitcast.325), channel_id=1, replica_groups=mesh['rows'=64,'cols'=4] {'rows'}, dimensions={0} | all-to-all | bytes 4194304 | tf_op jit(solution)/shard_map/all_to_all | solution.py:86
  211.7 2.7 fusion.31
  215.8 41.5 %all-reduce.8.cloned.1.call-done = f32[8,32,256]{2,0,1:T(8,128)} async-done(((f32[8,32,256]{2,0,1:T(8,128)}), f32[8,32,256]{2,0,1:T(8,128)}) %all-reduce.8.cloned.1.call-update) | async-done | bytes 262160 | tf_op jit(solution)/shard_map/psum | solution.py:96
  259.2 249.0 %all-reduce.4 = (f32[2048]{0:T(1024)S(1)}, f32[2048]{0:T(1024)S(1)}) all-reduce(f32[2048]{0:T(1024)S(1)} %dynamic-update-slice, f32[2048]{0:T(1024)S(1)} %dynamic-update-slice.1), channel_id=2, replica_groups=mesh['rows'=64,'cols'=4] {'rows'}, use_global_device_ids=true, to_apply=%add | all-reduce | flops 4096 | bytes 32768
  510.1 126.1 %all-reduce.2 = f32[2048]{0:T(1024)S(1)} all-reduce(f32[2048]{0:T(1024)S(1)} %dynamic-update-slice.2), channel_id=4, replica_groups=mesh['rows'=64,'cols'=4] {'rows'}, use_global_device_ids=true, to_apply=%add.2 | all-reduce | flops 2048 | bytes 16384
  638.2 32.0 %all_to_all.37 = bf16[64,1,32,256]{3,2,1,0:T(8,128)(2,1)S(1)} all-to-all(bf16[64,1,32,256]{3,2,1,0:T(8,128)(2,1)S(1)} %fusion.38), channel_id=1, replica_groups=mesh['rows'=64,'cols'=4] {'rows'}, dimensions={0} | all-to-all | bytes 2097152 | tf_op jit(solution)/shard_map/all_to_all | solution.py:63
  672.4 16.1 %while.44 = (s32[]{:T(128)}, f32[2,4,32,256]{3,2,1,0:T(8,128)S(1)}, f32[2,24,32,256]{3,2,1,0:T(8,128)}, bf16[2,24,32,256]{3,2,1,0:T(8,128)(2,1)S(1)}, pred[2,24]...) while((s32[]{:T(128)}, f32[2,4,32,256]{3,2,1,0:T(8,128)S(1)}, ...), condition=%wide.region_30.31_spmd, body=%wide.region_26.30_spmd.sunk | while | flops 274375680 | bytes 14607621 | solution.py:142
  672.6 5.1 select_convert_fusion.5
  680.6 5.1 select_convert_fusion.5
  685.9 1.5 fusion.123
  688.8 5.1 scatter_fusion.1
  693.9 57.7 %all_to_all.36 = f32[64,1,32,256]{3,2,1,0:T(8,128)S(1)} all-to-all(f32[64,1,32,256]{3,2,1,0:T(8,128)S(1)} %bitcast.324), channel_id=1, replica_groups=mesh['rows'=64,'cols'=4] {'rows'}, dimensions={0} | all-to-all | bytes 4194304 | tf_op jit(solution)/shard_map/all_to_all | solution.py:86
  751.6 2.7 fusion.34
  754.3 42.9 %all-reduce.10.cloned.1.call-done = f32[8,32,256]{2,0,1:T(8,128)} async-done(((f32[8,32,256]{2,0,1:T(8,128)}), f32[8,32,256]{2,0,1:T(8,128)}) %all-reduce.10.cloned.1.call-update) | async-done | bytes 262160 | tf_op jit(solution)/shard_map/psum | solution.py:96
  799.0 129.0 %all-reduce.3 = f32[2048]{0:T(1024)S(1)} all-reduce(f32[2048]{0:T(1024)S(1)} %dynamic-update-slice.3), channel_id=5, replica_groups=mesh['rows'=64,'cols'=4] {'rows'}, use_global_device_ids=true, to_apply=%add.3 | all-reduce | flops 2048 | bytes 16384
  (165 shorter events, 35.6 us)
Async XLA Ops:
  7.2 31.9 %copy-start.5 = (s32[8,6]{1,0:T(8,128)S(1)}, s32[8,6]{1,0:T(8,128)}, u32[]{:S(2)}) copy-start(s32[8,6]{1,0:T(8,128)} %param.9) | copy-start | bytes 580
  11.4 21.4 %all-to-all-start = ((s32[64,1,2]{2,1,0:T(1,128)}), s32[64,1,2]{2,1,0:T(1,128)S(1)}, u32[]{:S(2)}, u32[]{:S(2)}) async-start(s32[64,1,2]{2,1,0:T(1,128)} %copy.22), calls=%async_computation | async-start | bytes 65536 | tf_op jit(solution)/shard_map/all_to_all | solution.py:52
  34.4 21.8 %all-to-all-start.1 = ((bf16[64,1,16,256]{3,2,1,0:T(8,128)(2,1)}), bf16[64,1,16,256]{3,2,1,0:T(8,128)(2,1)S(1)}, u32[]{:S(2)}, u32[]{:S(2)}) async-start(bf16[64,1,16,256]{3,2,1,0:T(8,128)(2,1)} %bitcast_select_fusion.2), calls=%async_computation.1 | async-start | bytes 1048576 | tf_op jit(solution)/shard_map/all_to_all | solution.py:63
  56.9 20.4 %copy-start.4 = (f32[32,2048]{1,0:T(8,128)S(1)}, f32[32,2048]{1,0:T(8,128)}, u32[]{:S(2)}) copy-start(f32[32,2048]{1,0:T(8,128)} %param.11) | copy-start | bytes 786436
  70.9 16.1 %all-to-all-start.2 = ((f32[64,1,1,256]{3,2,1,0:T(1,128)}), f32[64,1,1,256]{3,2,1,0:T(1,128)S(1)}, u32[]{:S(2)}, u32[]{:S(2)}) async-start(f32[64,1,1,256]{3,2,1,0:T(1,128)} %reshape.432), calls=%async_computation.2 | async-start | bytes 131072 | tf_op jit(solution)/shard_map/all_to_all | solution.py:86
  77.4 20.1 %copy-start = (f32[4,8,8,256]{3,2,1,0:T(8,128)}, f32[4,8,8,256]{3,2,1,0:T(8,128)S(1)}, u32[]{:S(2)}) copy-start(f32[4,8,8,256]{3,2,1,0:T(8,128)S(1)} %copy.55) | copy-start | bytes 786436
  97.5 32.8 %all-to-all-start.3 = ((bf16[64,1,32,256]{3,2,1,0:T(8,128)(2,1)}), bf16[64,1,32,256]{3,2,1,0:T(8,128)(2,1)S(1)}, u32[]{:S(2)}, u32[]{:S(2)}) async-start(bf16[64,1,32,256]{3,2,1,0:T(8,128)(2,1)} %fusion.39), calls=%async_computation.3 | async-start | bytes 2097152 | tf_op jit(solution)/shard_map/all_to_all | solution.py:63
  102.2 155.1 %all-reduce.8.cloned.1.call-start = ((), (), s32[]{:S(2)}) async-start(), calls=%async_computation.7 | async-start | bytes 524288 | tf_op jit(solution)/shard_map/psum | solution.py:96
  154.0 60.4 %copy-start.6 = (u32[256]{0:T(256)S(1)}, u32[256]{0:T(256)}, u32[]{:S(2)}) copy-start(u32[256]{0:T(256)} %constant.223) | copy-start | bytes 3076
  154.0 103.3 %copy-start.1 = (f32[4,8,8,256]{3,2,1,0:T(8,128)S(1)}, f32[4,8,8,256]{3,2,1,0:T(8,128)}, u32[]{:S(2)}) copy-start(f32[4,8,8,256]{3,2,1,0:T(8,128)} %copy-done) | copy-start | bytes 786436
  214.4 582.8 %all-reduce.10.cloned.1.call-start = ((), (), s32[]{:S(2)}) async-start(), calls=%async_computation.8 | async-start | bytes 524288 | tf_op jit(solution)/shard_map/psum | solution.py:96
  693.9 103.3 %copy-start.2 = (f32[4,8,8,256]{3,2,1,0:T(8,128)S(1)}, f32[4,8,8,256]{3,2,1,0:T(8,128)}, u32[]{:S(2)}) copy-start(f32[4,8,8,256]{3,2,1,0:T(8,128)} %copy-done) | copy-start | bytes 786436
  693.9 103.3 %copy-start.3 = (f32[8,32,256]{2,0,1:T(8,128)S(1)}, f32[8,32,256]{2,0,1:T(8,128)}, u32[]{:S(2)}) copy-start(f32[8,32,256]{2,0,1:T(8,128)} %all-reduce.8.cloned.1.call-done) | copy-start | bytes 786436
Sparse Core Ops, SparseCore 0:
  214.5 42.7 all-reduce.7
  754.4 42.7 all-reduce.9
